TPU v7x, 128 devices: a whole 4x4x4 slice. The times are simulated.
128 devices in a mesh: row: 8 (over z, x_lo), col: 16 (over x_hi, y, core).
Axes of the slice: x: 4 (x_hi: 2, x_lo: 2; x = x_hi * 2 + x_lo), y: 4, z: 4, core: 2. Of those that a mesh axis runs over, the one named last changes fastest.
Arguments:
- t2_pairs: bfloat16 [8, 8, 16, 16, 64, 64], P('row', None, None, None, 'col'), may hold values from -6 to 6
- cycle_ints: bfloat16 [8192, 8192], P('row', 'col'), may hold values from -0.1875 to 0.1875
- eps_occ: float32 [8, 16], replicated, may hold values from -2 to -0.4
- eps_virt: float32 [8, 64], replicated, may hold values from 0.2 to 3
- occ_count: int32 [8], replicated, may hold values from 8 to 16, as said below
- virt_count: int32 [8], replicated, may hold values from 32 to 64, as said below
- window_irrep: int32 [1], replicated, may hold values from 0 to 7
Outputs:
- update: float32 [8192, 8192], P('row', 'col')
Inputs may be any that keep to these rules, and one draw needn't show every extreme that they name: `occ_count`: at least half of the slots; one irrep fills all 16, and another holds exactly the least. `virt_count`: at least half of the slots; one irrep fills all 64, and another holds exactly the least.
All inputs are finite; a program needn't handle non-finite values.
Results may differ from a plain program's by a relative error of at most 0.0003.
Values may be sent and summed in bfloat16 or wider, within the bound.
A program may use at most 128 MiB of HBM per device.

v0:
```python
import jax
import jax.numpy as jnp
from jax import lax
from jax.sharding import PartitionSpec as P

NIRREP = 8
OCC_CAP = 16
VIR_CAP = 64


def ph_vectors(eps_occ, eps_virt, occ_count, virt_count, window_irrep):
    irreps = jnp.arange(NIRREP, dtype=jnp.int32)
    partner = jnp.bitwise_xor(irreps, window_irrep[0])
    onehot = partner[:, None] == irreps[None, :]
    virt_rows = jnp.dot(onehot.astype(jnp.float32), eps_virt, precision=lax.Precision.HIGHEST)
    virt_live = jnp.sum(jnp.where(onehot, virt_count[None, :], 0), axis=1)
    energy = eps_occ[:, None, :] - virt_rows[:, :, None]
    slots_occ = jnp.arange(OCC_CAP, dtype=jnp.int32)
    slots_virt = jnp.arange(VIR_CAP, dtype=jnp.int32)
    live = (slots_occ[None, None, :] < occ_count[:, None, None]) & (
        slots_virt[None, :, None] < virt_live[:, None, None]
    )
    return (energy, live)


def per_device(t2_pairs, cycle_ints, eps_occ, eps_virt, occ_count, virt_count, window_irrep):
    irrep_local = t2_pairs.shape[0]
    virt_local = t2_pairs.shape[4]
    total = NIRREP * VIR_CAP * OCC_CAP
    energy, live = ph_vectors(eps_occ, eps_virt, occ_count, virt_count, window_irrep)
    row_index = lax.axis_index("row")
    col_index = lax.axis_index("col")
    first_irrep = row_index * irrep_local
    first_virt = col_index * virt_local
    zero_index = jnp.int32(0)
    source_live = lax.dynamic_slice(
        live, (first_irrep, first_virt, zero_index), (irrep_local, virt_local, OCC_CAP)
    )
    full_live = live.reshape(-1)
    ordered = jnp.transpose(t2_pairs, (0, 4, 2, 1, 5, 3)).reshape(
        irrep_local, virt_local, OCC_CAP, total
    )
    keep = source_live[:, :, :, None] & full_live[None, None, None, :]
    ordered = jnp.where(keep, ordered, jnp.zeros_like(ordered))
    moved = lax.all_to_all(ordered, "col", split_axis=3, concat_axis=1, tiled=True)
    amp_local = moved.reshape(irrep_local * VIR_CAP * OCC_CAP, moved.shape[3])
    amp_panel = lax.all_gather(amp_local, "row", axis=0, tiled=True)
    ints_panel = lax.all_gather(cycle_ints, "col", axis=1, tiled=True)
    cycle = jnp.dot(ints_panel, amp_panel, preferred_element_type=jnp.float32)
    rows_here = cycle.shape[0]
    cols_here = cycle.shape[1]
    flat_energy = energy.reshape(-1)
    row_start = row_index * rows_here
    col_start = col_index * cols_here
    row_energy = lax.dynamic_slice_in_dim(flat_energy, row_start, rows_here, 0)
    col_energy = lax.dynamic_slice_in_dim(flat_energy, col_start, cols_here, 0)
    row_live = lax.dynamic_slice_in_dim(full_live, row_start, rows_here, 0)
    col_live = lax.dynamic_slice_in_dim(full_live, col_start, cols_here, 0)
    denom = row_energy[:, None] + col_energy[None, :]
    return jnp.where(row_live[:, None] & col_live[None, :], cycle / denom, jnp.float32(0.0))


def solution(mesh):
    placed = (P("row", None, None, None, "col", None), P("row", "col"), P(), P(), P(), P(), P())
    return jax.shard_map(
        per_device, mesh=mesh, in_specs=placed, out_specs=P("row", "col"), check_vma=False
    )
```

profile of v0, /device:TPU:1, one launch (start us, length us, event | category | flops | bytes accessed | tf_op | source)
XLA Modules:
  0.0 408.3 jit_solution(13650713026373814684)
XLA Ops:
  7.2 0.8 select_reduce_fusion
  8.1 0.1 iota_compare_fusion.2
  8.1 0.7 iota_compare_fusion.3
  8.9 0.1 broadcast_and_fusion
  9.0 0.1 and.62
  9.2 7.9 %copy.20 = bf16[1,4,16,8,64,16]{5,4,3,2,1,0:T(8,128)(2,1)} copy(bf16[1,4,16,8,64,16]{4,1,5,2,3,0:T(4,128)(2,1)} %bitcast.23) | data formatting | bytes 2097152 | tf_op jit(solution)/shard_map/transpose | solution.py:40
  17.0 15.1 %reshape.106 = bf16[1,4,16,8192]{3,2,1,0:T(8,128)(2,1)S(1)} reshape(bf16[1,4,16,8,64,16]{5,4,3,2,1,0:T(8,128)(2,1)} %copy.20) | data formatting | bytes 2097152 | tf_op jit(solution)/shard_map/reshape | solution.py:40
  32.2 0.4 and_select_fusion
  32.6 8.3 %copy.21 = bf16[1,4,16,8192]{2,1,0,3:T(4,128)(2,1)} copy(bf16[1,4,16,8192]{3,2,1,0:T(8,128)(2,1)S(1)} %and_select_fusion) | data formatting | bytes 2097152 | tf_op jit(solution)/shard_map/jit(_where)/select_n | solution.py:44
  40.9 10.4 %reshape.108 = bf16[16,2,16384]{2,1,0:T(2,128)(2,1)S(1)} reshape(bf16[8192,1,4,16]{3,2,1,0:T(4,128)(2,1)} %bitcast.19) | data formatting | bytes 2097152
  51.3 25.2 %all_to_all.15 = bf16[16,2,16384]{2,1,0:T(2,128)(2,1)S(1)} all-to-all(bf16[16,2,16384]{2,1,0:T(2,128)(2,1)S(1)} %reshape.108), channel_id=1, replica_groups=mesh['row'=8,'col'=16] {'col'}, dimensions={0} | all-to-all | bytes 2097152 | tf_op jit(solution)/shard_map/all_to_all | solution.py:45
  76.5 7.5 %reshape.109 = bf16[8192,1,4,16]{3,2,1,0:T(4,128)(2,1)} reshape(bf16[16,2,16384]{2,1,0:T(2,128)(2,1)S(1)} %all_to_all.15) | data formatting | bytes 2097152
  84.0 8.6 %copy.25 = bf16[1,4,16,16,512]{4,3,2,1,0:T(8,128)(2,1)S(1)} copy(bf16[1,4,16,16,512]{2,1,4,3,0:T(4,128)(2,1)} %bitcast.20) | data formatting | bytes 2097152 | tf_op jit(solution)/shard_map/all_to_all | solution.py:45
  92.6 1.5 copy.23
  94.3 0.7 all-gather.5.cloned.1.call-update
  95.0 0.1 dynamic_slice.16
  95.0 0.2 fusion.1
  95.2 0.1 broadcast_subtract_fusion
  95.4 0.1 sub.20
  95.5 0.1 dynamic_slice.19
  95.6 165.7 %all-gather.3.cloned.1.call-done = bf16[8192,512]{1,0:T(8,128)(2,1)} async-done(((bf16[1024,512]{1,0:T(8,128)(2,1)}), bf16[8192,512]{1,0:T(8,128)(2,1)}) %all-gather.3.cloned.1.call-update) | async-done | bytes 8388624 | tf_op jit(solution)/shard_map/all_gather | solution.py:47
  261.3 122.6 %all-gather.5.cloned.1.call-done = bf16[1024,8192]{1,0:T(8,128)(2,1)} async-done(((bf16[1024,512]{1,0:T(8,128)(2,1)}), bf16[1024,8192]{1,0:T(8,128)(2,1)}) %all-gather.5.cloned.1.call-update) | async-done | bytes 16777232 | tf_op jit(solution)/shard_map/all_gather | solution.py:48
  383.9 15.7 %fusion = f32[1024,512]{0,1:T(8,128)S(1)} fusion(bf16[8192,512]{1,0:T(8,128)(2,1)} %all-gather.3.cloned.1.call-done, bf16[1024,8192]{1,0:T(8,128)(2,1)} %all-gather.5.cloned.1.call-done, f32[512]{0:T(512)S(1)} %dynamic_slice.19, f32[1024]{0:T(1024)S(1)} %dynamic_slice.18, pred[1024]{0:T(1024)(128)(4,1)S(1)} %dynamic_slice.15, ...), kind=kOutput, calls=%fused_computation.1 | convolution fusion | flops 8592031744 | bytes 27270656 | tf_op jit(solution)/shard_map/dot_general | solution.py:49
  399.6 1.8 copy.24
  (11 shorter events, 0.1 us)
Async XLA Ops:
  6.5 88.5 %copy-start = (f32[8,64]{1,0:T(8,128)S(1)}, f32[8,64]{1,0:T(8,128)}, u32[]{:S(2)}) copy-start(f32[8,64]{1,0:T(8,128)} %param.10) | copy-start | bytes 6148
  6.5 254.8 %all-gather.3.cloned.1.call-start = ((), (), s32[]{:S(2)}) async-start(), calls=%async_computation.1 | async-start | bytes 9437184 | tf_op jit(solution)/shard_map/all_gather | solution.py:47
  84.0 11.2 %copy-start.1 = (f32[8,16]{1,0:T(8,128)S(1)}, f32[8,16]{1,0:T(8,128)}, u32[]{:S(2)}) copy-start(f32[8,16]{1,0:T(8,128)} %param.9) | copy-start | bytes 1540
  94.2 289.7 %all-gather.5.cloned.1.call-start = ((), (), s32[]{:S(2)}) async-start(), calls=%async_computation.2 | async-start | bytes 17825792 | tf_op jit(solution)/shard_map/all_gather | solution.py:48
Sparse Core Ops, SparseCore 0:
  94.3 166.9 all-gather.2
  263.6 120.3 all-gather.4
where the time goes:
time: 409 us; the launch traced here: 408 us
  waiting for transfers between devices  289 us (71%)
  local copies, waits for them, and re-layouts  61.7 us (15%)
  blocking collectives  25.2 us (6%)
  matrix products  15.9 us (4%)
  between operations  14.2 us (3%)
    all_gather x1, waiting for transfers between devices, per_device(): amp_panel = lax.all_gather(amp_local, 'row', axis=0, tiled=True)  166 us
    all_gather x1, waiting for transfers between devices, per_device(): ints_panel = lax.all_gather(cycle_ints, 'col', axis=1, tiled=True)  123 us
    all_to_all x1, blocking collectives, per_device(): lax.all_to_all(ordered, 'col', split_axis=3, concat_axis=1, tiled=True)  25.2 us
    unnamed x6, local copies, waits for them, and re-layouts  18 us
    dot_general x1, matrix products, per_device(): cycle = jnp.dot(ints_panel, amp_panel, preferred_element_type=jnp.float32)  15.7 us
    reshape x1, local copies, waits for them, and re-layouts, per_device(): jnp.transpose(t2_pairs, (0, 4, 2, 1, 5, 3))  15.1 us
    all_to_all x2, local copies, waits for them, and re-layouts, per_device(): lax.all_to_all(ordered, 'col', split_axis=3, concat_axis=1, tiled=True)  10.1 us
    select_n x1, local copies, waits for them, and re-layouts, per_device(): ordered = jnp.where(keep, ordered, jnp.zeros_like(ordered))  8.33 us
  transfers between devices with their start and end apart: 2, of which 2 were waited for; matrix products, arithmetic and copies ran while one was open for 0% of the time, Pallas kernels for 0%

commit v1 on v0

--- a/solution.py
+++ b/solution.py
@@ -45,7 +45,8 @@
     moved = lax.all_to_all(ordered, "col", split_axis=3, concat_axis=1, tiled=True)
     amp_local = moved.reshape(irrep_local * VIR_CAP * OCC_CAP, moved.shape[3])
     amp_panel = lax.all_gather(amp_local, "row", axis=0, tiled=True)
-    ints_panel = lax.all_gather(cycle_ints, "col", axis=1, tiled=True)
+    outgoing = jnp.stack([cycle_ints] * lax.axis_size("col"))
+    ints_panel = jnp.concatenate(lax.all_to_all(outgoing, "col", 0, 0), axis=1)
     cycle = jnp.dot(ints_panel, amp_panel, preferred_element_type=jnp.float32)
     rows_here = cycle.shape[0]
     cols_here = cycle.shape[1]

time: 409 us -> 455 us (1.11)
  waiting for transfers between devices: 289 us -> 338 us
  blocking collectives: 25.2 us -> 0 us
  starting transfers between devices: 0.04 us -> 14.3 us
  local copies, waits for them, and re-layouts: 61.7 us -> 69 us
    all_gather x1, waiting for transfers between devices: 166 us -> 322 us  [per_device(): amp_panel = lax.all_gather(amp_local, 'row', axis=0, tiled=True)]
    all_gather x1 -> x0, waiting for transfers between devices: 123 us -> none  [per_device(): ints_panel = lax.all_gather(cycle_ints, 'col', axis=1, tiled=True)]
    all_to_all x1 -> x0, blocking collectives: 25.2 us -> none  [per_device(): lax.all_to_all(ordered, 'col', split_axis=3, concat_axis=1, tiled=True)]
    all_to_all x0 -> x2, waiting for transfers between devices: none -> 16.7 us  [the longest x1 16.7 us: per_device(): lax.all_to_all(ordered, 'col', split_axis=3, concat_axis=1, tiled=True)]
    all_to_all x0 -> x2, starting transfers between devices: none -> 14.2 us  [the longest x1 8.45 us: per_device(): lax.all_to_all(ordered, 'col', split_axis=3, concat_axis=1, tiled=True)]
    another operation x0 -> x1, local copies, waits for them, and re-layouts: none -> 5.92 us  [per_device(): outgoing = jnp.stack([cycle_ints] * lax.axis_size('col'))]
    unnamed x6 -> x9, local copies, waits for them, and re-layouts: 18 us -> 19.3 us
  transfers between devices with their start and end apart: 2 -> 3, of which waited for: 2 -> 2; matrix products, arithmetic and copies ran while one was open for 0% -> 4% of each run, Pallas kernels for 0% -> 0%
where the time goes in v1:
time: 455 us; the launch traced here: 454 us
  waiting for transfers between devices  338 us (74%)
  local copies, waits for them, and re-layouts  69 us (15%)
  matrix products  15.8 us (3%)
  starting transfers between devices  14.3 us (3%)
  between operations  14.2 us (3%)
    all_gather x1, waiting for transfers between devices, per_device(): amp_panel = lax.all_gather(amp_local, 'row', axis=0, tiled=True)  322 us
    unnamed x9, local copies, waits for them, and re-layouts  19.3 us
    all_to_all x1, waiting for transfers between devices, per_device(): lax.all_to_all(ordered, 'col', split_axis=3, concat_axis=1, tiled=True)  16.7 us
    dot_general x1, matrix products, per_device(): cycle = jnp.dot(ints_panel, amp_panel, preferred_element_type=jnp.float32)  15.6 us
    reshape x1, local copies, waits for them, and re-layouts, per_device(): jnp.transpose(t2_pairs, (0, 4, 2, 1, 5, 3))  15.1 us
    all_to_all x2, local copies, waits for them, and re-layouts, per_device(): lax.all_to_all(ordered, 'col', split_axis=3, concat_axis=1, tiled=True)  10.1 us
  transfers between devices with their start and end apart: 3, of which 2 were waited for; matrix products, arithmetic and copies ran while one was open for 4% of the time, Pallas kernels for 0%

profile of v1, /device:TPU:1, one launch (start us, length us, event | category | flops | bytes accessed | tf_op | source)
XLA Modules:
  0.0 453.9 jit_solution(9335281621856569683)
XLA Ops:
  7.2 0.8 select_reduce_fusion
  8.1 0.7 iota_compare_fusion.3
  8.9 0.1 broadcast_and_fusion
  9.0 0.1 and.62
  9.2 7.9 %copy.23 = bf16[1,4,16,8,64,16]{5,4,3,2,1,0:T(8,128)(2,1)} copy(bf16[1,4,16,8,64,16]{4,1,5,2,3,0:T(4,128)(2,1)} %bitcast.26) | data formatting | bytes 2097152 | tf_op jit(solution)/shard_map/transpose | solution.py:40
  17.0 15.1 %reshape.114 = bf16[1,4,16,8192]{3,2,1,0:T(8,128)(2,1)S(1)} reshape(bf16[1,4,16,8,64,16]{5,4,3,2,1,0:T(8,128)(2,1)} %copy.23) | data formatting | bytes 2097152 | tf_op jit(solution)/shard_map/reshape | solution.py:40
  32.2 0.4 and_select_fusion
  32.6 8.3 %copy.24 = bf16[1,4,16,8192]{2,1,0,3:T(4,128)(2,1)} copy(bf16[1,4,16,8192]{3,2,1,0:T(8,128)(2,1)S(1)} %and_select_fusion) | data formatting | bytes 2097152 | tf_op jit(solution)/shard_map/jit(_where)/select_n | solution.py:44
  40.9 11.2 %reshape.118 = bf16[16,2,16384]{2,1,0:T(2,128)(2,1)} reshape(bf16[8192,1,4,16]{3,2,1,0:T(4,128)(2,1)} %bitcast.22) | data formatting | bytes 2097152
  52.2 8.4 %all-to-all-start = ((bf16[16,2,16384]{2,1,0:T(2,128)(2,1)}), bf16[16,2,16384]{2,1,0:T(2,128)(2,1)S(1)}, u32[]{:S(2)}, u32[]{:S(2)}) async-start(bf16[16,2,16384]{2,1,0:T(2,128)(2,1)} %reshape.118), calls=%async_computation | async-start | bytes 2097152 | tf_op jit(solution)/shard_map/all_to_all | solution.py:45
  60.6 0.5 copy.27
  61.2 16.7 %all-to-all-done = bf16[16,2,16384]{2,1,0:T(2,128)(2,1)S(1)} async-done(((bf16[16,2,16384]{2,1,0:T(2,128)(2,1)}), bf16[16,2,16384]{2,1,0:T(2,128)(2,1)S(1)}, u32[]{:S(2)}, u32[]{:S(2)}) %all-to-all-start) | async-done | bytes 1048608 | tf_op jit(solution)/shard_map/all_to_all | solution.py:45
  77.8 5.9 %stack.2 = bf16[16,1024,512]{1,2,0:T(8,128)(2,1)} broadcast(bf16[1024,512]{0,1:T(8,128)(2,1)S(1)} %copy.27), dimensions={1,2} | broadcast | bytes 17825792 | tf_op jit(solution)/shard_map/stack | solution.py:48
  83.7 5.8 %all-to-all-start.1 = ((bf16[16,1024,512]{1,2,0:T(8,128)(2,1)}), bf16[16,1024,512]{1,2,0:T(8,128)(2,1)}, u32[]{:S(2)}, u32[]{:S(2)}) async-start(bf16[16,1024,512]{1,2,0:T(8,128)(2,1)} %stack.2), calls=%async_computation.1 | async-start | bytes 33554432 | tf_op jit(solution)/shard_map/all_to_all | solution.py:49
  89.5 7.5 %reshape.119 = bf16[8192,1,4,16]{3,2,1,0:T(4,128)(2,1)} reshape(bf16[16,2,16384]{2,1,0:T(2,128)(2,1)S(1)} %all-to-all-done) | data formatting | bytes 2097152
  97.1 8.6 %copy.29 = bf16[1,4,16,16,512]{4,3,2,1,0:T(8,128)(2,1)S(1)} copy(bf16[1,4,16,16,512]{2,1,4,3,0:T(4,128)(2,1)} %bitcast.23) | data formatting | bytes 2097152 | tf_op jit(solution)/shard_map/all_to_all | solution.py:45
  105.7 1.5 copy.26
  107.3 0.1 dynamic_slice.16
  107.4 0.2 fusion.1
  107.5 0.1 broadcast_subtract_fusion
  107.7 0.1 sub.20
  107.9 321.7 %all-gather.2.cloned.1.call-done = bf16[8192,512]{1,0:T(8,128)(2,1)} async-done(((bf16[1024,512]{1,0:T(8,128)(2,1)}), bf16[8192,512]{1,0:T(8,128)(2,1)}) %all-gather.2.cloned.1.call-update) | async-done | bytes 8388624 | tf_op jit(solution)/shard_map/all_gather | solution.py:47
  429.6 15.6 %fusion = f32[1024,512]{0,1:T(8,128)S(1)} fusion(bf16[8192,512]{1,0:T(8,128)(2,1)} %all-gather.2.cloned.1.call-done, bf16[1024,8192]{0,1:T(8,128)(2,1)} %bitcast.7, f32[512]{0:T(512)S(1)} %dynamic_slice.19, f32[1024]{0:T(1024)S(1)} %dynamic_slice.18, pred[1024]{0:T(1024)(128)(4,1)S(1)} %dynamic_slice.15, pred[512]{0:T(512)(128)(4,1)S(1)} %dynamic_slice.16), kind=kOutput, calls=%fused_computation.1 | convolution fusion | flops 8592031744 | bytes 27270656 | tf_op jit(solution)/shard_map/dot_general | solution.py:50
  445.2 1.8 copy.28
  (15 shorter events, 0.3 us)
Async XLA Ops:
  6.5 100.8 %copy-start = (f32[8,64]{1,0:T(8,128)S(1)}, f32[8,64]{1,0:T(8,128)}, u32[]{:S(2)}) copy-start(f32[8,64]{1,0:T(8,128)} %param.10) | copy-start | bytes 6148
  32.6 28.0 %copy-start.1 = (bf16[1024,512]{1,0:T(8,128)(2,1)S(1)}, bf16[1024,512]{1,0:T(8,128)(2,1)}, u32[]{:S(2)}) copy-start(bf16[1024,512]{1,0:T(8,128)(2,1)} %param.8) | copy-start | bytes 3145732
  52.2 25.7 %all-to-all-start = ((bf16[16,2,16384]{2,1,0:T(2,128)(2,1)}), bf16[16,2,16384]{2,1,0:T(2,128)(2,1)S(1)}, u32[]{:S(2)}, u32[]{:S(2)}) async-start(bf16[16,2,16384]{2,1,0:T(2,128)(2,1)} %reshape.118), calls=%async_computation | async-start | bytes 2097152 | tf_op jit(solution)/shard_map/all_to_all | solution.py:45
  83.7 345.8 %all-to-all-start.1 = ((bf16[16,1024,512]{1,2,0:T(8,128)(2,1)}), bf16[16,1024,512]{1,2,0:T(8,128)(2,1)}, u32[]{:S(2)}, u32[]{:S(2)}) async-start(bf16[16,1024,512]{1,2,0:T(8,128)(2,1)} %stack.2), calls=%async_computation.1 | async-start | bytes 33554432 | tf_op jit(solution)/shard_map/all_to_all | solution.py:49
  89.5 340.1 %all-gather.2.cloned.1.call-start = ((), (), s32[]{:S(2)}) async-start(), calls=%async_computation.2 | async-start | bytes 9437184 | tf_op jit(solution)/shard_map/all_gather | solution.py:47
  97.1 10.5 %copy-start.2 = (f32[8,16]{1,0:T(8,128)S(1)}, f32[8,16]{1,0:T(8,128)}, u32[]{:S(2)}) copy-start(f32[8,16]{1,0:T(8,128)} %param.9) | copy-start | bytes 1540
Sparse Core Ops, SparseCore 0:
  107.4 322.1 all-gather.1

commit v2 on v0

--- a/solution.py
+++ b/solution.py
@@ -6,6 +6,13 @@
 NIRREP = 8
 OCC_CAP = 16
 VIR_CAP = 64
+
+
+def swap_blocks(x, name, split, join):
+    count = lax.axis_size(name)
+    blocks = jnp.stack(jnp.split(x, count, axis=split), axis=0)
+    blocks = lax.all_to_all(blocks, name, split_axis=0, concat_axis=0)
+    return jnp.concatenate(blocks, axis=join)
 
 
 def ph_vectors(eps_occ, eps_virt, occ_count, virt_count, window_irrep):
@@ -42,7 +49,7 @@
     )
     keep = source_live[:, :, :, None] & full_live[None, None, None, :]
     ordered = jnp.where(keep, ordered, jnp.zeros_like(ordered))
-    moved = lax.all_to_all(ordered, "col", split_axis=3, concat_axis=1, tiled=True)
+    moved = swap_blocks(ordered, "col", 3, 1)
     amp_local = moved.reshape(irrep_local * VIR_CAP * OCC_CAP, moved.shape[3])
     amp_panel = lax.all_gather(amp_local, "row", axis=0, tiled=True)
     ints_panel = lax.all_gather(cycle_ints, "col", axis=1, tiled=True)

time: 409 us -> 373 us (0.912)
  local copies, waits for them, and re-layouts: 61.7 us -> 25.4 us
    unnamed x6 -> x19, local copies, waits for them, and re-layouts: 18 us -> 0.11 us
    all_to_all x2 -> x0, local copies, waits for them, and re-layouts: 10.1 us -> none  [per_device(): lax.all_to_all(ordered, 'col', split_axis=3, concat_axis=1, tiled=True)]
    select_n x1 -> x0, local copies, waits for them, and re-layouts: 8.33 us -> none  [per_device(): ordered = jnp.where(keep, ordered, jnp.zeros_like(ordered))]
where the time goes in v2:
time: 373 us; the launch traced here: 372 us
  waiting for transfers between devices  289 us (77%)
  local copies, waits for them, and re-layouts  25.4 us (7%)
  blocking collectives  25.3 us (7%)
  matrix products  15.9 us (4%)
  between operations  14.3 us (4%)
    all_gather x1, waiting for transfers between devices, per_device(): amp_panel = lax.all_gather(amp_local, 'row', axis=0, tiled=True)  166 us
    all_gather x1, waiting for transfers between devices, per_device(): ints_panel = lax.all_gather(cycle_ints, 'col', axis=1, tiled=True)  123 us
    all_to_all x1, blocking collectives, swap_blocks(): blocks = lax.all_to_all(blocks, name, split_axis=0, concat_axis=0)  25.3 us
    dot_general x1, matrix products, per_device(): cycle = jnp.dot(ints_panel, amp_panel, preferred_element_type=jnp.float32)  15.7 us
    reshape x1, local copies, waits for them, and re-layouts, per_device(): jnp.transpose(t2_pairs, (0, 4, 2, 1, 5, 3))  15.1 us
    transpose x1, local copies, waits for them, and re-layouts, per_device(): jnp.transpose(t2_pairs, (0, 4, 2, 1, 5, 3))  7.88 us
  transfers between devices with their start and end apart: 2, of which 2 were waited for; matrix products, arithmetic and copies ran while one was open for 0% of the time, Pallas kernels for 0%

profile of v2, /device:TPU:1, one launch (start us, length us, event | category | flops | bytes accessed | tf_op | source)
XLA Modules:
  0.0 372.2 jit_solution(2108434927644377425)
XLA Ops:
  6.5 0.0 copy-start
  7.2 0.8 select_reduce_fusion
  8.1 0.1 iota_compare_fusion.2
  8.1 0.7 iota_compare_fusion.3
  8.9 0.1 broadcast_and_fusion
  9.0 0.1 and.62
  9.2 7.9 %copy.11 = bf16[1,4,16,8,64,16]{5,4,3,2,1,0:T(8,128)(2,1)} copy(bf16[1,4,16,8,64,16]{4,1,5,2,3,0:T(4,128)(2,1)} %bitcast.80) | data formatting | bytes 2097152 | tf_op jit(solution)/shard_map/transpose | solution.py:47
  17.0 15.1 %reshape.102 = bf16[1,4,16,8192]{3,2,1,0:T(8,128)(2,1)S(1)} reshape(bf16[1,4,16,8,64,16]{5,4,3,2,1,0:T(8,128)(2,1)} %copy.11) | data formatting | bytes 2097152 | tf_op jit(solution)/shard_map/reshape | solution.py:47
  32.2 0.4 and_select_fusion
  32.8 0.0 copy-start.1
  32.8 25.3 %all_to_all.5 = bf16[16,1,4,16,512]{4,3,2,1,0:T(8,128)(2,1)} all-to-all(bf16[16,1,4,16,512]{4,3,2,1,0:T(8,128)(2,1)S(1)} %fusion.1), channel_id=1, replica_groups=mesh['row'=8,'col'=16] {'col'}, dimensions={0} | all-to-all | bytes 2097152 | tf_op jit(solution)/shard_map/all_to_all | solution.py:14
  58.1 0.0 all-gather.3.cloned.1.call-update
  58.1 0.0 all-gather.5.cloned.1.call-start
  58.2 0.7 all-gather.5.cloned.1.call-update
  58.9 0.1 dynamic_slice.16
  59.0 0.0 copy-done
  59.0 0.2 fusion.17
  59.1 0.1 broadcast_subtract_fusion
  59.3 0.1 sub.20
  59.4 0.1 dynamic_slice.19
  59.5 165.7 %all-gather.3.cloned.1.call-done = bf16[8192,512]{1,0:T(8,128)(2,1)} async-done(((bf16[1024,512]{1,0:T(8,128)(2,1)}), bf16[8192,512]{1,0:T(8,128)(2,1)}) %all-gather.3.cloned.1.call-update) | async-done | bytes 8388624 | tf_op jit(solution)/shard_map/all_gather | solution.py:54
  225.2 122.6 %all-gather.5.cloned.1.call-done = bf16[1024,8192]{1,0:T(8,128)(2,1)} async-done(((bf16[1024,512]{1,0:T(8,128)(2,1)}), bf16[1024,8192]{1,0:T(8,128)(2,1)}) %all-gather.5.cloned.1.call-update) | async-done | bytes 16777232 | tf_op jit(solution)/shard_map/all_gather | solution.py:55
  347.9 15.7 %fusion = f32[1024,512]{0,1:T(8,128)S(1)} fusion(bf16[8192,512]{1,0:T(8,128)(2,1)} %all-gather.3.cloned.1.call-done, bf16[1024,8192]{1,0:T(8,128)(2,1)} %all-gather.5.cloned.1.call-done, f32[512]{0:T(512)S(1)} %dynamic_slice.19, f32[1024]{0:T(1024)S(1)} %dynamic_slice.18, pred[1024]{0:T(1024)(128)(4,1)S(1)} %dynamic_slice.15, ...), kind=kOutput, calls=%fused_computation.1 | convolution fusion | flops 8592031744 | bytes 27270656 | tf_op jit(solution)/shard_map/dot_general | solution.py:56
  363.6 1.8 copy.12
  (22 shorter events, 0.1 us)
Async XLA Ops:
  6.5 52.4 %copy-start = (f32[8,64]{1,0:T(8,128)S(1)}, f32[8,64]{1,0:T(8,128)}, u32[]{:S(2)}) copy-start(f32[8,64]{1,0:T(8,128)} %param.10) | copy-start | bytes 6148
  6.5 218.7 %all-gather.3.cloned.1.call-start = ((), (), s32[]{:S(2)}) async-start(), calls=%async_computation.1 | async-start | bytes 9437184 | tf_op jit(solution)/shard_map/all_gather | solution.py:54
  32.8 26.3 %copy-start.1 = (f32[8,16]{1,0:T(8,128)S(1)}, f32[8,16]{1,0:T(8,128)}, u32[]{:S(2)}) copy-start(f32[8,16]{1,0:T(8,128)} %param.9) | copy-start | bytes 1540
  58.1 289.7 %all-gather.5.cloned.1.call-start = ((), (), s32[]{:S(2)}) async-start(), calls=%async_computation.2 | async-start | bytes 17825792 | tf_op jit(solution)/shard_map/all_gather | solution.py:55
Sparse Core Ops, SparseCore 0:
  58.2 166.9 all-gather.2
  227.5 120.3 all-gather.4
